TPU v7x, 512 devices: a whole 4x8x8 slice. The times are simulated.
512 devices in a mesh: dp: 4 (over x), expert: 128 (over z, y, core).
Axes of the slice: x: 4, y: 8, z: 8, core: 2. Of those that a mesh axis runs over, the one named last changes fastest.
Arguments:
- x_rows: bfloat16 [65536, 1024], P(('dp', 'expert')), may hold values from -6 to 6
- expert_ids: int32 [65536, 1], P(('dp', 'expert')), may hold values from 0 to 127; in each aligned block of 128 rows (0 to 127, 128 to 255, ...) at most 2 rows name the same one
- gates: float32 [65536, 1], P(('dp', 'expert')), may hold values from 0.1 to 1
- cotangent: bfloat16 [65536, 1024], P(('dp', 'expert')), may hold values from -6 to 6
- w_gate: bfloat16 [128, 1024, 384], P('expert', 'dp'), may hold values from -0.1875 to 0.1875
- w_up: bfloat16 [128, 1024, 384], P('expert', 'dp'), may hold values from -0.1875 to 0.1875
- w_down: bfloat16 [128, 384, 1024], P('expert', None, 'dp'), may hold values from -0.3125 to 0.3125
Outputs:
- gated_out: bfloat16 [65536, 1024], P(('dp', 'expert'))
- input_grad: bfloat16 [65536, 1024], P(('dp', 'expert'))
- gate_grad: float32 [65536, 1], P(('dp', 'expert'))
- grad_gate: bfloat16 [128, 1024, 384], P('expert', 'dp')
- grad_up: bfloat16 [128, 1024, 384], P('expert', 'dp')
- grad_down: bfloat16 [128, 384, 1024], P('expert', None, 'dp')
Inputs may be any that keep to these rules, and one draw needn't show every extreme that they name: `expert_ids`: among the rows of one device each expert id occurs at most 2 times, and in some device's rows some expert occurs exactly 2 times.
All inputs are finite; a program needn't handle non-finite values.
Results may differ from a plain program's by a relative error of at most 0.009.
Values may be sent and summed in bfloat16 or wider, within the bound.
No kernel may reach another device: no remote copies, remote signals or barrier semaphores. Data moves between devices by JAX's collectives and lax.ppermute only.
A program may use at most 64 MiB of HBM per device.

v0:
```python
import jax
import jax.numpy as jnp
from jax import lax
from jax.sharding import PartitionSpec as P


def expert_rows(rows_in, rows_scaled, proj_gate, proj_up, proj_down):
    gate_act = jnp.dot(rows_in, proj_gate, preferred_element_type=jnp.float32)
    up_act = jnp.dot(rows_in, proj_up, preferred_element_type=jnp.float32)
    sigma = jax.nn.sigmoid(gate_act)
    hidden = (gate_act * sigma * up_act).astype(jnp.bfloat16)
    result = jnp.dot(hidden, proj_down, preferred_element_type=jnp.float32).astype(jnp.bfloat16)
    backed = jnp.dot(rows_scaled, proj_down.T, preferred_element_type=jnp.float32)
    d_gate_act = (backed * up_act * sigma * (1.0 + gate_act * (1.0 - sigma))).astype(jnp.bfloat16)
    d_up_act = (backed * gate_act * sigma).astype(jnp.bfloat16)
    d_input = (
        jnp.dot(d_gate_act, proj_gate.T, preferred_element_type=jnp.float32)
        + jnp.dot(d_up_act, proj_up.T, preferred_element_type=jnp.float32)
    ).astype(jnp.bfloat16)
    grad_g = jnp.dot(rows_in.T, d_gate_act, preferred_element_type=jnp.float32)
    grad_u = jnp.dot(rows_in.T, d_up_act, preferred_element_type=jnp.float32)
    grad_d = jnp.dot(hidden.T, rows_scaled, preferred_element_type=jnp.float32)
    return (result, d_input, (grad_g, grad_u, grad_d), (hidden, d_gate_act, d_up_act))


def per_device(x_rows, expert_ids, gates, cotangent, w_gate, w_up, w_down):
    full_gate, full_up, full_down = (
        lax.all_gather(w_gate, "dp", axis=1, tiled=True),
        lax.all_gather(w_up, "dp", axis=1, tiled=True),
        lax.all_gather(w_down, "dp", axis=2, tiled=True),
    )
    proj_gate = full_gate[0]
    proj_up = full_up[0]
    proj_down = full_down[0]
    experts = lax.axis_size("expert")
    row_count = x_rows.shape[0]
    width = x_rows.shape[1]
    capacity = 2 * row_count // experts
    row_ids = expert_ids[:, 0]
    onehot = (row_ids[:, None] == jnp.arange(experts, dtype=jnp.int32)[None, :]).astype(jnp.int32)
    ranking = jnp.sum((jnp.cumsum(onehot, 0) - onehot) * onehot, 1)
    slot = row_ids * capacity + ranking
    counts = jnp.sum(onehot, 0)
    scaled = (gates * cotangent.astype(jnp.float32)).astype(jnp.bfloat16)
    send_in = (
        jnp.zeros((experts * capacity, width), jnp.bfloat16)
        .at[slot]
        .set(x_rows)
        .reshape(experts, capacity, width)
    )
    send_scaled = (
        jnp.zeros((experts * capacity, width), jnp.bfloat16)
        .at[slot]
        .set(scaled)
        .reshape(experts, capacity, width)
    )
    recv_in, recv_scaled, recv_counts = (
        lax.all_to_all(send_in, "expert", split_axis=0, concat_axis=0, tiled=True),
        lax.all_to_all(send_scaled, "expert", split_axis=0, concat_axis=0, tiled=True),
        lax.all_to_all(
            counts.reshape(experts, 1), "expert", split_axis=0, concat_axis=0, tiled=True
        ),
    )
    flat_in = recv_in.reshape(experts * capacity, width)
    flat_scaled = recv_scaled.reshape(experts * capacity, width)
    slot_out, slot_grad, grads, acts = expert_rows(
        flat_in, flat_scaled, proj_gate, proj_up, proj_down
    )
    back_result, back_input = (
        lax.all_to_all(
            slot_out.reshape(experts, capacity, width),
            "expert",
            split_axis=0,
            concat_axis=0,
            tiled=True,
        ),
        lax.all_to_all(
            slot_grad.reshape(experts, capacity, width),
            "expert",
            split_axis=0,
            concat_axis=0,
            tiled=True,
        ),
    )
    row_out = back_result.reshape(experts * capacity, width)[slot]
    input_grad = back_input.reshape(experts * capacity, width)[slot]
    gated_out = (gates * row_out.astype(jnp.float32)).astype(jnp.bfloat16)
    gate_grad = jnp.sum(
        cotangent.astype(jnp.float32) * row_out.astype(jnp.float32), 1, keepdims=True
    )
    summed_gate, summed_up, summed_down = (
        lax.psum_scatter(
            grads[0][None].astype(jnp.bfloat16), "dp", scatter_dimension=1, tiled=True
        ).astype(jnp.float32),
        lax.psum_scatter(
            grads[1][None].astype(jnp.bfloat16), "dp", scatter_dimension=1, tiled=True
        ).astype(jnp.float32),
        lax.psum_scatter(
            grads[2][None].astype(jnp.bfloat16), "dp", scatter_dimension=2, tiled=True
        ).astype(jnp.float32),
    )
    return (
        gated_out,
        input_grad,
        gate_grad,
        summed_gate.astype(jnp.bfloat16),
        summed_up.astype(jnp.bfloat16),
        summed_down.astype(jnp.bfloat16),
    )


def solution(mesh):
    in_specs = (
        P(("dp", "expert"), None),
        P(("dp", "expert"), None),
        P(("dp", "expert"), None),
        P(("dp", "expert"), None),
        P("expert", "dp", None),
        P("expert", "dp", None),
        P("expert", None, "dp"),
    )
    out_specs = (
        P(("dp", "expert"), None),
        P(("dp", "expert"), None),
        P(("dp", "expert"), None),
        P("expert", "dp", None),
        P("expert", "dp", None),
        P("expert", None, "dp"),
    )
    return jax.shard_map(
        per_device, mesh=mesh, in_specs=in_specs, out_specs=out_specs, check_vma=False
    )
```

profile of v0, /device:TPU:8, one launch (start us, length us, event | category | flops | bytes accessed | tf_op | source)
XLA Modules:
  0.0 194.1 jit_solution(5530824760676524770)
XLA Ops:
  7.2 0.7 fusion.23
  8.1 0.8 select_reduce_fusion
  8.9 0.7 fusion.24
  9.6 1.7 scatter_custom_fusion
  11.3 1.0 reshape.40
  12.3 17.4 %all-to-all-start = ((bf16[128,2,1024]{2,1,0:T(2,128)(2,1)}), bf16[128,2,1024]{2,1,0:T(2,128)(2,1)S(1)}, u32[]{:S(2)}, u32[]{:S(2)}) async-start(bf16[128,2,1024]{2,1,0:T(2,128)(2,1)} %reshape.40), calls=%async_computation | async-start | bytes 1048576 | tf_op jit(solution)/shard_map/all_to_all | solution.py:58
  29.7 1.4 scatter_custom_fusion.1
  31.1 1.0 reshape.44
  32.1 14.0 %all_gather.9 = bf16[1,1024,384]{2,1,0:T(8,128)(2,1)S(1)} all-gather(bf16[1,256,384]{2,1,0:T(8,128)(2,1)S(1)} %copy-done.6), channel_id=1, replica_groups=mesh['dp'=4,'expert'=128] {'dp'}, dimensions={1}, use_global_device_ids=true | all-gather | bytes 983040 | tf_op jit(solution)/shard_map/all_gather | solution.py:28
  46.1 3.8 %all-to-all-done = bf16[128,2,1024]{2,1,0:T(2,128)(2,1)S(1)} async-done(((bf16[128,2,1024]{2,1,0:T(2,128)(2,1)}), bf16[128,2,1024]{2,1,0:T(2,128)(2,1)S(1)}, u32[]{:S(2)}, u32[]{:S(2)}) %all-to-all-start) | async-done | bytes 524320 | tf_op jit(solution)/shard_map/all_to_all | solution.py:58
  49.9 10.5 %all-to-all-start.2 = ((bf16[128,2,1024]{2,1,0:T(2,128)(2,1)}), bf16[128,2,1024]{2,1,0:T(2,128)(2,1)}, u32[]{:S(2)}, u32[]{:S(2)}) async-start(bf16[128,2,1024]{2,1,0:T(2,128)(2,1)} %reshape.44), calls=%async_computation.2 | async-start | bytes 1048576 | tf_op jit(solution)/shard_map/all_to_all | solution.py:59
  60.5 13.7 %all_gather.10 = bf16[1,1024,384]{2,1,0:T(8,128)(2,1)S(1)} all-gather(bf16[1,256,384]{2,1,0:T(8,128)(2,1)S(1)} %copy-done.7), channel_id=1, replica_groups=mesh['dp'=4,'expert'=128] {'dp'}, dimensions={1}, use_global_device_ids=true | all-gather | bytes 983040 | tf_op jit(solution)/shard_map/all_gather | solution.py:29
  74.2 14.3 %all_gather.11 = bf16[1,384,1024]{2,1,0:T(8,128)(2,1)S(1)} all-gather(bf16[1,384,256]{2,1,0:T(8,128)(2,1)S(1)} %copy-done.8), channel_id=1, replica_groups=mesh['dp'=4,'expert'=128] {'dp'}, dimensions={2}, use_global_device_ids=true | all-gather | bytes 983040 | tf_op jit(solution)/shard_map/all_gather | solution.py:30
  88.7 1.2 fusion.12
  89.9 1.2 fusion.8
  91.1 1.2 reshape.45
  92.3 2.4 %multiply_convert_fusion = (bf16[256,384]{1,0:T(8,128)(2,1)}, bf16[256,384]{1,0:T(8,128)(2,1)S(1)}, bf16[256,384]{1,0:T(8,128)(2,1)}) fusion(f32[256,384]{1,0:T(8,128)} %fusion.12, f32[256,384]{1,0:T(8,128)} %fusion.8, bf16[256,1024]{1,0:T(8,128)(2,1)S(1)} %reshape.45, bf16[1,384,1024]{2,1,0:T(8,128)(2,1)S(1)} %all_gather.11), kind=kOutput, calls=%fused_computation.29 | convolution fusion | flops 202899456 | bytes 2686976 | tf_op jit(solution)/shard_map/dot_general | solution.py:13
  94.7 0.7 copy-done.4
  95.4 1.3 fusion
  96.8 2.3 %fusion.1 = bf16[1,1024,384]{2,1,0:T(8,128)(2,1)} fusion(bf16[256,1024]{1,0:T(8,128)(2,1)S(1)} %reshape.41, bf16[256,384]{1,0:T(8,128)(2,1)} %get-tuple-element.6), kind=kOutput, calls=%fused_computation.10 | convolution fusion | flops 201719808 | bytes 1507328 | tf_op jit(solution)/shard_map/dot_general | solution.py:21
  99.1 1.4 convolution_convert_fusion.3
  100.5 1.0 reshape.42
  101.5 13.8 %all-to-all-start.1 = ((bf16[128,2,1024]{2,1,0:T(2,128)(2,1)}), bf16[128,2,1024]{2,1,0:T(2,128)(2,1)S(1)}, u32[]{:S(2)}, u32[]{:S(2)}) async-start(bf16[128,2,1024]{2,1,0:T(2,128)(2,1)} %reshape.42), calls=%async_computation.1 | async-start | bytes 1048576 | tf_op jit(solution)/shard_map/all_to_all | solution.py:70
  115.5 1.3 fusion.2
  118.2 1.0 reshape.46
  119.2 16.2 %all-to-all-done.1 = bf16[128,2,1024]{2,1,0:T(2,128)(2,1)S(1)} async-done(((bf16[128,2,1024]{2,1,0:T(2,128)(2,1)}), bf16[128,2,1024]{2,1,0:T(2,128)(2,1)S(1)}, u32[]{:S(2)}, u32[]{:S(2)}) %all-to-all-start.1) | async-done | bytes 524320 | tf_op jit(solution)/shard_map/all_to_all | solution.py:70
  135.4 5.8 %all-to-all-start.3 = ((bf16[128,2,1024]{2,1,0:T(2,128)(2,1)}), bf16[128,2,1024]{2,1,0:T(2,128)(2,1)S(1)}, u32[]{:S(2)}, u32[]{:S(2)}) async-start(bf16[128,2,1024]{2,1,0:T(2,128)(2,1)} %reshape.46), calls=%async_computation.3 | async-start | bytes 1048576 | tf_op jit(solution)/shard_map/all_to_all | solution.py:77
  141.4 0.9 gather_fusion
  142.3 19.1 %all-to-all-done.3 = bf16[128,2,1024]{2,1,0:T(2,128)(2,1)S(1)} async-done(((bf16[128,2,1024]{2,1,0:T(2,128)(2,1)}), bf16[128,2,1024]{2,1,0:T(2,128)(2,1)S(1)}, u32[]{:S(2)}, u32[]{:S(2)}) %all-to-all-start.3) | async-done | bytes 524320 | tf_op jit(solution)/shard_map/all_to_all | solution.py:77
  161.6 1.6 gather_fusion.1
  163.2 1.3 fusion.16
  164.5 23.1 %reduce-scatter.8.cloned.1.call-done = bf16[1,384,256]{2,1,0:T(8,128)(2,1)} async-done(((bf16[1,384,1024]{2,1,0:T(8,128)(2,1)}), bf16[1,384,256]{2,1,0:T(8,128)(2,1)}) %reduce-scatter.8.cloned.1.call-update) | async-done | bytes 196624 | tf_op jit(solution)/shard_map/reduce_scatter | solution.py:98
  (35 shorter events, 2.6 us)
Async XLA Ops:
  11.3 18.4 %copy-start = (bf16[128,1024]{1,0:T(8,128)(2,1)S(1)}, bf16[128,1024]{1,0:T(8,128)(2,1)}, u32[]{:S(2)}) copy-start(bf16[128,1024]{1,0:T(8,128)(2,1)} %param.10) | copy-start | bytes 786436
  11.3 18.4 %copy-start.9 = (f32[128,1]{0,1:T(1,128)S(1)}, f32[128,1]{0,1:T(1,128)}, u32[]{:S(2)}) copy-start(f32[128,1]{0,1:T(1,128)} %param.9) | copy-start | bytes 1540
  12.3 37.6 %all-to-all-start = ((bf16[128,2,1024]{2,1,0:T(2,128)(2,1)}), bf16[128,2,1024]{2,1,0:T(2,128)(2,1)S(1)}, u32[]{:S(2)}, u32[]{:S(2)}) async-start(bf16[128,2,1024]{2,1,0:T(2,128)(2,1)} %reshape.40), calls=%async_computation | async-start | bytes 1048576 | tf_op jit(solution)/shard_map/all_to_all | solution.py:58
  29.7 2.4 %copy-start.6 = (bf16[1,256,384]{2,1,0:T(8,128)(2,1)S(1)}, bf16[1,256,384]{2,1,0:T(8,128)(2,1)}, u32[]{:S(2)}) copy-start(bf16[1,256,384]{2,1,0:T(8,128)(2,1)} %param.11) | copy-start | bytes 589828
  32.1 28.4 %copy-start.7 = (bf16[1,256,384]{2,1,0:T(8,128)(2,1)S(1)}, bf16[1,256,384]{2,1,0:T(8,128)(2,1)}, u32[]{:S(2)}) copy-start(bf16[1,256,384]{2,1,0:T(8,128)(2,1)} %param.12) | copy-start | bytes 589828
  46.1 28.1 %copy-start.8 = (bf16[1,384,256]{2,1,0:T(8,128)(2,1)S(1)}, bf16[1,384,256]{2,1,0:T(8,128)(2,1)}, u32[]{:S(2)}) copy-start(bf16[1,384,256]{2,1,0:T(8,128)(2,1)} %param.13) | copy-start | bytes 589828
  49.9 41.2 %all-to-all-start.2 = ((bf16[128,2,1024]{2,1,0:T(2,128)(2,1)}), bf16[128,2,1024]{2,1,0:T(2,128)(2,1)}, u32[]{:S(2)}, u32[]{:S(2)}) async-start(bf16[128,2,1024]{2,1,0:T(2,128)(2,1)} %reshape.44), calls=%async_computation.2 | async-start | bytes 1048576 | tf_op jit(solution)/shard_map/all_to_all | solution.py:59
  60.4 104.1 %reduce-scatter.4.cloned.1.call-start = ((), (), s32[]{:S(2)}) async-start(), calls=%async_computation.7 | async-start | bytes 983040 | tf_op jit(solution)/shard_map/reduce_scatter | solution.py:92
  94.7 0.7 copy-start.4
  96.7 67.8 %reduce-scatter.6.cloned.1.call-start = ((), (), s32[]{:S(2)}) async-start(), calls=%async_computation.8 | async-start | bytes 983040 | tf_op jit(solution)/shard_map/reduce_scatter | solution.py:95
  100.5 15.0 %copy-start.3 = (bf16[256,384]{1,0:T(8,128)(2,1)S(1)}, bf16[256,384]{1,0:T(8,128)(2,1)}, u32[]{:S(2)}) copy-start(bf16[256,384]{1,0:T(8,128)(2,1)} %get-tuple-element.8) | copy-start | bytes 589828
  101.5 34.0 %all-to-all-start.1 = ((bf16[128,2,1024]{2,1,0:T(2,128)(2,1)}), bf16[128,2,1024]{2,1,0:T(2,128)(2,1)S(1)}, u32[]{:S(2)}, u32[]{:S(2)}) async-start(bf16[128,2,1024]{2,1,0:T(2,128)(2,1)} %reshape.42), calls=%async_computation.1 | async-start | bytes 1048576 | tf_op jit(solution)/shard_map/all_to_all | solution.py:70
  115.3 1.6 copy-start.5
  115.3 72.3 %reduce-scatter.8.cloned.1.call-start = ((), (), s32[]{:S(2)}) async-start(), calls=%async_computation.9 | async-start | bytes 983040 | tf_op jit(solution)/shard_map/reduce_scatter | solution.py:98
  116.8 0.9 copy-start.2
  135.4 26.0 %all-to-all-start.3 = ((bf16[128,2,1024]{2,1,0:T(2,128)(2,1)}), bf16[128,2,1024]{2,1,0:T(2,128)(2,1)S(1)}, u32[]{:S(2)}, u32[]{:S(2)}) async-start(bf16[128,2,1024]{2,1,0:T(2,128)(2,1)} %reshape.46), calls=%async_computation.3 | async-start | bytes 1048576 | tf_op jit(solution)/shard_map/all_to_all | solution.py:77
  161.6 1.6 copy-start.1
Sparse Core Ops, SparseCore 0:
  96.9 28.3 reduce-scatter.3
  128.7 27.6 reduce-scatter.5
  159.8 27.7 reduce-scatter.7
where the time goes:
time: 195 us; the launch traced here: 194 us
  waiting for transfers between devices  62.2 us (32%)
  starting transfers between devices  47.7 us (24%)
  blocking collectives  42 us (22%)
  between operations  14 us (7%)
  matrix products  12 us (6%)
  local copies, waits for them, and re-layouts  11.1 us (6%)
  other arithmetic  5.11 us (3%)
    reduce_scatter x1, waiting for transfers between devices, per_device(): lax.psum_scatter(grads[2][None].astype(jnp.bfloat16), 'dp', scatter_dimen...  23.1 us
    all_to_all x1, waiting for transfers between devices, per_device(): lax.all_to_all(slot_grad.reshape(experts, capacity, width), 'expert', spl...  19.1 us
    all_to_all x1, starting transfers between devices, per_device(): lax.all_to_all(send_in, 'expert', split_axis=0, concat_axis=0, tiled=True)  17.4 us
    all_to_all x1, waiting for transfers between devices, per_device(): lax.all_to_all(slot_out.reshape(experts, capacity, width), 'expert', spli...  16.2 us
    all_gather x1, blocking collectives, per_device(): lax.all_gather(w_down, 'dp', axis=2, tiled=True)  14.3 us
    all_gather x1, blocking collectives, per_device(): lax.all_gather(w_gate, 'dp', axis=1, tiled=True)  14 us
    all_to_all x1, starting transfers between devices, per_device(): lax.all_to_all(slot_out.reshape(experts, capacity, width), 'expert', spli...  13.8 us
    all_gather x1, blocking collectives, per_device(): lax.all_gather(w_up, 'dp', axis=1, tiled=True)  13.7 us
  transfers between devices with their start and end apart: 7, of which 4 were waited for; matrix products, arithmetic and copies ran while one was open for 9% of the time, Pallas kernels for 0%

commit v1 on v0

--- a/solution.py
+++ b/solution.py
@@ -2,6 +2,16 @@
 import jax.numpy as jnp
 from jax import lax
 from jax.sharding import PartitionSpec as P
+
+
+def meet_floor_all(arr_in, axis_name):
+    arr_now = jnp.concatenate(
+        lax.all_to_all(
+            jnp.stack(tuple((arr_in for _ in range(lax.axis_size(axis_name))))), axis_name, 0, 0
+        ),
+        axis=1,
+    )
+    return arr_now
 
 
 def expert_rows(rows_in, rows_scaled, proj_gate, proj_up, proj_down):
@@ -25,7 +35,7 @@
 
 def per_device(x_rows, expert_ids, gates, cotangent, w_gate, w_up, w_down):
     full_gate, full_up, full_down = (
-        lax.all_gather(w_gate, "dp", axis=1, tiled=True),
+        meet_floor_all(w_gate, "dp"),
         lax.all_gather(w_up, "dp", axis=1, tiled=True),
         lax.all_gather(w_down, "dp", axis=2, tiled=True),
     )

time: 195 us -> 202 us (1.036)
  waiting for transfers between devices: 62.2 us -> 84.5 us
  blocking collectives: 42 us -> 27.6 us
    all_gather x1 -> x0, blocking collectives: 14 us -> none  [per_device(): lax.all_gather(w_gate, 'dp', axis=1, tiled=True)]
    all_to_all x1, waiting for transfers between devices: 3.8 us -> 17.8 us  [per_device(): lax.all_to_all(send_in, 'expert', split_axis=0, concat_axis=0, tiled=True)]
    all_to_all x0 -> x1, waiting for transfers between devices: none -> 9.07 us  [meet_floor_all(): lax.all_to_all(jnp.stack(tuple((arr_in for _ in range(lax.axis_size(axis_...]
    all_to_all x0 -> x1, starting transfers between devices: none -> 4.29 us  [meet_floor_all(): lax.all_to_all(jnp.stack(tuple((arr_in for _ in range(lax.axis_size(axis_...]
    all_to_all x1, starting transfers between devices: 10.5 us -> 6.42 us  [per_device(): lax.all_to_all(send_scaled, 'expert', split_axis=0, concat_axis=0, tiled=...]
  transfers between devices with their start and end apart: 7 -> 8, of which waited for: 4 -> 5; matrix products, arithmetic and copies ran while one was open for 9% -> 10% of each run, Pallas kernels for 0% -> 0%
where the time goes in v1:
time: 202 us
  waiting for transfers between devices  84.5 us (42%)
  starting transfers between devices  47.5 us (24%)
  blocking collectives  27.6 us (14%)
  between operations  14 us (7%)
  local copies, waits for them, and re-layouts  13 us (6%)
  matrix products  12 us (6%)
  other arithmetic  3.14 us (2%)
    reduce_scatter x1, waiting for transfers between devices, per_device(): lax.psum_scatter(grads[2][None].astype(jnp.bfloat16), 'dp', scatter_dimen...  22.3 us
    all_to_all x1, waiting for transfers between devices, per_device(): lax.all_to_all(slot_grad.reshape(experts, capacity, width), 'expert', spl...  19.1 us
    all_to_all x1, waiting for transfers between devices, per_device(): lax.all_to_all(send_in, 'expert', split_axis=0, concat_axis=0, tiled=True)  17.8 us
    all_to_all x1, starting transfers between devices, per_device(): lax.all_to_all(send_in, 'expert', split_axis=0, concat_axis=0, tiled=True)  17.4 us
    all_to_all x1, waiting for transfers between devices, per_device(): lax.all_to_all(slot_out.reshape(experts, capacity, width), 'expert', spli...  16.2 us
    all_gather x1, blocking collectives, per_device(): lax.all_gather(w_down, 'dp', axis=2, tiled=True)  14.1 us
    all_gather x1, blocking collectives, per_device(): lax.all_gather(w_up, 'dp', axis=1, tiled=True)  13.5 us
    all_to_all x1, starting transfers between devices, per_device(): lax.all_to_all(slot_out.reshape(experts, capacity, width), 'expert', spli...  13.3 us
  transfers between devices with their start and end apart: 8, of which 5 were waited for; matrix products, arithmetic and copies ran while one was open for 10% of the time, Pallas kernels for 0%

profile of v1, /device:TPU:8, one launch (start us, length us, event | category | flops | bytes accessed | tf_op | source)
XLA Modules:
  0.0 201.8 jit_solution(14055251979376128768)
XLA Ops:
  7.2 1.9 stack.2
  9.1 4.3 %all-to-all-start.1 = ((bf16[4,1,256,384]{3,2,1,0:T(8,128)(2,1)}), bf16[4,1,256,384]{3,2,1,0:T(8,128)(2,1)S(1)}, u32[]{:S(2)}, u32[]{:S(2)}) async-start(bf16[4,1,256,384]{3,2,1,0:T(8,128)(2,1)} %stack.2), calls=%async_computation.1 | async-start | bytes 1572864 | tf_op jit(solution)/shard_map/all_to_all | solution.py:9
  13.8 1.7 scatter_custom_fusion
  15.6 1.0 reshape.43
  16.6 9.1 %all-to-all-done.1 = bf16[4,1,256,384]{3,2,1,0:T(8,128)(2,1)S(1)} async-done(((bf16[4,1,256,384]{3,2,1,0:T(8,128)(2,1)}), bf16[4,1,256,384]{3,2,1,0:T(8,128)(2,1)S(1)}, u32[]{:S(2)}, u32[]{:S(2)}) %all-to-all-start.1) | async-done | bytes 786464 | tf_op jit(solution)/shard_map/all_to_all | solution.py:9
  25.6 17.4 %all-to-all-start = ((bf16[128,2,1024]{2,1,0:T(2,128)(2,1)}), bf16[128,2,1024]{2,1,0:T(2,128)(2,1)S(1)}, u32[]{:S(2)}, u32[]{:S(2)}) async-start(bf16[128,2,1024]{2,1,0:T(2,128)(2,1)} %reshape.43), calls=%async_computation | async-start | bytes 1048576 | tf_op jit(solution)/shard_map/all_to_all | solution.py:68
  43.0 1.4 scatter_custom_fusion.1
  44.4 1.0 reshape.47
  45.4 17.8 %all-to-all-done = bf16[128,2,1024]{2,1,0:T(2,128)(2,1)S(1)} async-done(((bf16[128,2,1024]{2,1,0:T(2,128)(2,1)}), bf16[128,2,1024]{2,1,0:T(2,128)(2,1)S(1)}, u32[]{:S(2)}, u32[]{:S(2)}) %all-to-all-start) | async-done | bytes 524320 | tf_op jit(solution)/shard_map/all_to_all | solution.py:68
  63.2 6.4 %all-to-all-start.3 = ((bf16[128,2,1024]{2,1,0:T(2,128)(2,1)}), bf16[128,2,1024]{2,1,0:T(2,128)(2,1)}, u32[]{:S(2)}, u32[]{:S(2)}) async-start(bf16[128,2,1024]{2,1,0:T(2,128)(2,1)} %reshape.47), calls=%async_computation.3 | async-start | bytes 1048576 | tf_op jit(solution)/shard_map/all_to_all | solution.py:69
  69.7 13.5 %all_gather.6 = bf16[1,1024,384]{2,1,0:T(8,128)(2,1)S(1)} all-gather(bf16[1,256,384]{2,1,0:T(8,128)(2,1)S(1)} %copy-done.6), channel_id=1, replica_groups=mesh['dp'=4,'expert'=128] {'dp'}, dimensions={1}, use_global_device_ids=true | all-gather | bytes 983040 | tf_op jit(solution)/shard_map/all_gather | solution.py:39
  83.2 14.1 %all_gather.7 = bf16[1,384,1024]{2,1,0:T(8,128)(2,1)S(1)} all-gather(bf16[1,384,256]{2,1,0:T(8,128)(2,1)S(1)} %copy-done.7), channel_id=1, replica_groups=mesh['dp'=4,'expert'=128] {'dp'}, dimensions={2}, use_global_device_ids=true | all-gather | bytes 983040 | tf_op jit(solution)/shard_map/all_gather | solution.py:40
  97.5 1.2 fusion.21
  98.7 1.2 fusion.8
  99.9 1.2 reshape.48
  101.2 2.4 %multiply_convert_fusion = (bf16[256,384]{1,0:T(8,128)(2,1)}, bf16[256,384]{1,0:T(8,128)(2,1)S(1)}, bf16[256,384]{1,0:T(8,128)(2,1)}) fusion(f32[256,384]{1,0:T(8,128)} %fusion.21, f32[256,384]{1,0:T(8,128)} %fusion.8, bf16[256,1024]{1,0:T(8,128)(2,1)S(1)} %reshape.48, bf16[1,384,1024]{2,1,0:T(8,128)(2,1)S(1)} %all_gather.7), kind=kOutput, calls=%fused_computation.25 | convolution fusion | flops 202899456 | bytes 2686976 | tf_op jit(solution)/shard_map/dot_general | solution.py:23
  103.5 0.7 copy-done.4
  104.2 1.4 fusion
  105.6 2.3 %fusion.1 = bf16[1,1024,384]{2,1,0:T(8,128)(2,1)} fusion(bf16[256,1024]{1,0:T(8,128)(2,1)S(1)} %reshape.44, bf16[256,384]{1,0:T(8,128)(2,1)} %get-tuple-element.6), kind=kOutput, calls=%fused_computation.10 | convolution fusion | flops 201719808 | bytes 1507328 | tf_op jit(solution)/shard_map/dot_general | solution.py:31
  108.0 1.4 convolution_convert_fusion.3
  109.4 1.0 reshape.45
  110.4 13.3 %all-to-all-start.2 = ((bf16[128,2,1024]{2,1,0:T(2,128)(2,1)}), bf16[128,2,1024]{2,1,0:T(2,128)(2,1)S(1)}, u32[]{:S(2)}, u32[]{:S(2)}) async-start(bf16[128,2,1024]{2,1,0:T(2,128)(2,1)} %reshape.45), calls=%async_computation.2 | async-start | bytes 1048576 | tf_op jit(solution)/shard_map/all_to_all | solution.py:80
  124.0 1.3 fusion.2
  126.2 0.5 fusion.3
  126.7 1.0 reshape.49
  127.7 16.2 %all-to-all-done.2 = bf16[128,2,1024]{2,1,0:T(2,128)(2,1)S(1)} async-done(((bf16[128,2,1024]{2,1,0:T(2,128)(2,1)}), bf16[128,2,1024]{2,1,0:T(2,128)(2,1)S(1)}, u32[]{:S(2)}, u32[]{:S(2)}) %all-to-all-start.2) | async-done | bytes 524320 | tf_op jit(solution)/shard_map/all_to_all | solution.py:80
  143.9 5.8 %all-to-all-start.4 = ((bf16[128,2,1024]{2,1,0:T(2,128)(2,1)}), bf16[128,2,1024]{2,1,0:T(2,128)(2,1)S(1)}, u32[]{:S(2)}, u32[]{:S(2)}) async-start(bf16[128,2,1024]{2,1,0:T(2,128)(2,1)} %reshape.49), calls=%async_computation.4 | async-start | bytes 1048576 | tf_op jit(solution)/shard_map/all_to_all | solution.py:87
  149.9 0.9 gather_fusion
  150.7 19.1 %all-to-all-done.4 = bf16[128,2,1024]{2,1,0:T(2,128)(2,1)S(1)} async-done(((bf16[128,2,1024]{2,1,0:T(2,128)(2,1)}), bf16[128,2,1024]{2,1,0:T(2,128)(2,1)S(1)}, u32[]{:S(2)}, u32[]{:S(2)}) %all-to-all-start.4) | async-done | bytes 524320 | tf_op jit(solution)/shard_map/all_to_all | solution.py:87
  170.1 1.6 gather_fusion.1
  171.6 1.3 fusion.12
  173.0 22.3 %reduce-scatter.8.cloned.1.call-done = bf16[1,384,256]{2,1,0:T(8,128)(2,1)} async-done(((bf16[1,384,1024]{2,1,0:T(8,128)(2,1)}), bf16[1,384,256]{2,1,0:T(8,128)(2,1)}) %reduce-scatter.8.cloned.1.call-update) | async-done | bytes 196624 | tf_op jit(solution)/shard_map/reduce_scatter | solution.py:108
  (37 shorter events, 2.4 us)
Async XLA Ops:
  7.2 6.2 %copy-start.8 = (s32[128,1]{0,1:T(1,128)S(1)}, s32[128,1]{0,1:T(1,128)}, u32[]{:S(2)}) copy-start(s32[128,1]{0,1:T(1,128)} %param.8) | copy-start | bytes 1540
  9.1 16.6 %all-to-all-start.1 = ((bf16[4,1,256,384]{3,2,1,0:T(8,128)(2,1)}), bf16[4,1,256,384]{3,2,1,0:T(8,128)(2,1)S(1)}, u32[]{:S(2)}, u32[]{:S(2)}) async-start(bf16[4,1,256,384]{3,2,1,0:T(8,128)(2,1)} %stack.2), calls=%async_computation.1 | async-start | bytes 1572864 | tf_op jit(solution)/shard_map/all_to_all | solution.py:9
  15.5 27.5 %copy-start = (bf16[128,1024]{1,0:T(8,128)(2,1)S(1)}, bf16[128,1024]{1,0:T(8,128)(2,1)}, u32[]{:S(2)}) copy-start(bf16[128,1024]{1,0:T(8,128)(2,1)} %param.10) | copy-start | bytes 786436
  15.5 27.5 %copy-start.9 = (f32[128,1]{0,1:T(1,128)S(1)}, f32[128,1]{0,1:T(1,128)}, u32[]{:S(2)}) copy-start(f32[128,1]{0,1:T(1,128)} %param.9) | copy-start | bytes 1540
  25.6 37.6 %all-to-all-start = ((bf16[128,2,1024]{2,1,0:T(2,128)(2,1)}), bf16[128,2,1024]{2,1,0:T(2,128)(2,1)S(1)}, u32[]{:S(2)}, u32[]{:S(2)}) async-start(bf16[128,2,1024]{2,1,0:T(2,128)(2,1)} %reshape.43), calls=%async_computation | async-start | bytes 1048576 | tf_op jit(solution)/shard_map/all_to_all | solution.py:68
  44.4 25.3 %copy-start.6 = (bf16[1,256,384]{2,1,0:T(8,128)(2,1)S(1)}, bf16[1,256,384]{2,1,0:T(8,128)(2,1)}, u32[]{:S(2)}) copy-start(bf16[1,256,384]{2,1,0:T(8,128)(2,1)} %param.12) | copy-start | bytes 589828
  45.4 37.8 %copy-start.7 = (bf16[1,384,256]{2,1,0:T(8,128)(2,1)S(1)}, bf16[1,384,256]{2,1,0:T(8,128)(2,1)}, u32[]{:S(2)}) copy-start(bf16[1,384,256]{2,1,0:T(8,128)(2,1)} %param.13) | copy-start | bytes 589828
  63.2 36.7 %all-to-all-start.3 = ((bf16[128,2,1024]{2,1,0:T(2,128)(2,1)}), bf16[128,2,1024]{2,1,0:T(2,128)(2,1)}, u32[]{:S(2)}, u32[]{:S(2)}) async-start(bf16[128,2,1024]{2,1,0:T(2,128)(2,1)} %reshape.47), calls=%async_computation.3 | async-start | bytes 1048576 | tf_op jit(solution)/shard_map/all_to_all | solution.py:69
  69.6 103.3 %reduce-scatter.4.cloned.1.call-start = ((), (), s32[]{:S(2)}) async-start(), calls=%async_computation.8 | async-start | bytes 983040 | tf_op jit(solution)/shard_map/reduce_scatter | solution.py:102
  103.5 0.7 copy-start.4
  105.6 67.4 %reduce-scatter.6.cloned.1.call-start = ((), (), s32[]{:S(2)}) async-start(), calls=%async_computation.9 | async-start | bytes 983040 | tf_op jit(solution)/shard_map/reduce_scatter | solution.py:105
  109.4 14.6 %copy-start.3 = (bf16[256,384]{1,0:T(8,128)(2,1)S(1)}, bf16[256,384]{1,0:T(8,128)(2,1)}, u32[]{:S(2)}) copy-start(bf16[256,384]{1,0:T(8,128)(2,1)} %get-tuple-element.8) | copy-start | bytes 589828
  110.4 33.5 %all-to-all-start.2 = ((bf16[128,2,1024]{2,1,0:T(2,128)(2,1)}), bf16[128,2,1024]{2,1,0:T(2,128)(2,1)S(1)}, u32[]{:S(2)}, u32[]{:S(2)}) async-start(bf16[128,2,1024]{2,1,0:T(2,128)(2,1)} %reshape.45), calls=%async_computation.2 | async-start | bytes 1048576 | tf_op jit(solution)/shard_map/all_to_all | solution.py:80
  123.7 1.5 copy-start.5
  123.7 71.5 %reduce-scatter.8.cloned.1.call-start = ((), (), s32[]{:S(2)}) async-start(), calls=%async_computation.10 | async-start | bytes 983040 | tf_op jit(solution)/shard_map/reduce_scatter | solution.py:108
  125.3 0.9 copy-start.2
  143.9 26.0 %all-to-all-start.4 = ((bf16[128,2,1024]{2,1,0:T(2,128)(2,1)}), bf16[128,2,1024]{2,1,0:T(2,128)(2,1)S(1)}, u32[]{:S(2)}, u32[]{:S(2)}) async-start(bf16[128,2,1024]{2,1,0:T(2,128)(2,1)} %reshape.49), calls=%async_computation.4 | async-start | bytes 1048576 | tf_op jit(solution)/shard_map/all_to_all | solution.py:87
  170.1 1.6 copy-start.1
Sparse Core Ops, SparseCore 0:
  105.7 27.2 reduce-scatter.3
  136.4 27.5 reduce-scatter.5
  167.5 27.7 reduce-scatter.7
